TPU v7x, 32 devices: a whole 2x2x4 slice. The times are simulated.
32 devices in a mesh: groups: 2 (over y), snap: 4 (over z), slab: 2 (over x), sub: 2 (over core).
Axes of the slice: x: 2, y: 2, z: 4, core: 2. Of those that a mesh axis runs over, the one named last changes fastest.
Arguments:
- fields: float32 [8, 4, 4, 16, 128], P(('groups', 'snap'), None, 'slab', 'sub'), parts along dimension 0, may hold values from -18 to 18
- snap_ids: int32 [8], P(('groups', 'snap')), parts along dimension 0, may hold values from 0 to 63
- snap_weight: float32 [64], replicated, may hold values from 0.5 to 2
- product_terms: int32 [192, 3], replicated, may hold values from 0 to 27, as said below
- mix_weight: float32 [192], replicated, may hold values from -1.5 to 1.5
Outputs:
- whitened: bfloat16 [8, 192, 4, 16, 128], P(('groups', 'snap'), None, 'slab', 'sub'), parts along dimension 0
- r_factor: float32 [384, 192], P('groups'), parts along dimension 0
There are 2 independent parts, one for each index of `groups`. A program takes and returns all parts, laid end to end along the dimension named above; an argument that names none is the same for every part. Nothing has to cross between parts.
Inputs may be any that keep to these rules, and one draw needn't show every extreme that they name: `product_terms`: each row names three different bases, and no two rows are equal.
All inputs are finite; a program needn't handle non-finite values.
Results may differ from a plain program's by a relative error of at most 0.0028.
Values sent between devices are 32-bit elements; how exact they have to be, the bound alone decides.
A program may use at most 64 MiB of HBM per device.

v0:
```python
import jax
import jax.numpy as jnp
from jax import lax
from jax.sharding import PartitionSpec as P

ridge_value = 0.05


def padded_2(block, sides, width):
    for axis, dim in sides:
        count = lax.axis_size(axis)
        forward = [(i, i + 1) for i in range(count - 1)]
        forward.append((count - 1, 0))
        backward = [(target, source) for source, target in forward]
        low = lax.ppermute(
            lax.slice_in_dim(block, block.shape[dim] - width, None, axis=dim), axis, forward
        )
        high = lax.ppermute(lax.slice_in_dim(block, 0, width, axis=dim), axis, backward)
        block = jnp.concatenate([low, block, high], axis=dim)
    return block


def stencil_pair(values, ahead_one, behind_one, ahead_two, behind_two):
    first_deriv = (8.0 * (ahead_one - behind_one) - (ahead_two - behind_two)) / 12.0
    second_deriv = (
        16.0 * (ahead_one + behind_one) - (ahead_two + behind_two) - 30.0 * values
    ) / 12.0
    return (first_deriv, second_deriv)


def dot_highest(left_matrix, right_matrix):
    return jnp.dot(left_matrix, right_matrix, precision=lax.Precision.HIGHEST)


def upper_cholesky(matrix):
    order = matrix.shape[0]
    positions = jnp.arange(order, dtype=jnp.int32)

    def column_step(step, state):
        work, upper = state
        row_now = lax.dynamic_slice_in_dim(work, step, 1, 0)[0]
        pivot = lax.dynamic_slice_in_dim(row_now, step, 1, 0)[0]
        scaled = jnp.where(positions >= step, row_now / jnp.sqrt(pivot), 0.0)
        work = work - scaled[:, None] * scaled[None, :]
        upper = lax.dynamic_update_slice_in_dim(upper, scaled[None, :], step, 0)
        return (work, upper)

    start = (matrix, jnp.zeros_like(matrix))
    return lax.fori_loop(0, order, column_step, start)[1]


def transposed_solve(upper, right_side):
    order = upper.shape[0]
    positions = jnp.arange(order, dtype=jnp.int32)

    def row_step(step, solved):
        column = lax.dynamic_slice_in_dim(upper, step, 1, 1)[:, 0]
        pivot = lax.dynamic_slice_in_dim(column, step, 1, 0)[0]
        masked = jnp.where(positions < step, column, 0.0)
        target = lax.dynamic_slice_in_dim(right_side, step, 1, 0)
        row_new = (target - dot_highest(masked[None, :], solved)) / pivot
        return lax.dynamic_update_slice_in_dim(solved, row_new, step, 0)

    return lax.fori_loop(0, order, row_step, jnp.zeros_like(right_side))


def local(fields, snap_ids, snap_weight, product_terms, mix_weight):
    padded = padded_2(fields, (("slab", 2), ("sub", 3)), 2)
    layers = fields.shape[2]
    columns = fields.shape[3]
    center = padded[0, :, 2 : 2 + layers, 2 : 2 + columns, :]

    def along_z(offset):
        return padded[0, :, 2 + offset : 2 + offset + layers, 2 : 2 + columns, :]

    def along_x(offset):
        return padded[0, :, 2 : 2 + layers, 2 + offset : 2 + offset + columns, :]

    z_first, z_second = stencil_pair(center, along_z(1), along_z(-1), along_z(2), along_z(-2))
    x_first, x_second = stencil_pair(center, along_x(1), along_x(-1), along_x(2), along_x(-2))
    y_first, y_second = stencil_pair(
        center,
        jnp.roll(center, -1, 3),
        jnp.roll(center, 1, 3),
        jnp.roll(center, -2, 3),
        jnp.roll(center, 2, 3),
    )
    stacked = jnp.stack([center, z_first, x_first, y_first, z_second, x_second, y_second], axis=1)
    base_count = stacked.shape[0] * stacked.shape[1]
    bases = stacked.reshape(base_count, -1)
    table_size = snap_weight.shape[0]
    snap_scale = jnp.sum(jnp.where(jnp.arange(table_size) == snap_ids[0], snap_weight, 0.0))
    feature_count = product_terms.shape[0]
    choose = (product_terms.T.reshape(-1)[:, None] == jnp.arange(base_count)[None, :]).astype(
        jnp.float32
    )
    picked = dot_highest(choose, bases)
    left_term = picked[:feature_count]
    middle = picked[feature_count : 2 * feature_count]
    right_term = picked[2 * feature_count :]
    features = snap_scale * left_term * (middle + mix_weight[:, None] * right_term)
    local_gram = lax.dot_general(
        features, features, (((1,), (1,)), ((), ())), precision=lax.Precision.HIGHEST
    )
    cells_total = float(
        lax.axis_size("snap") * lax.axis_size("slab") * lax.axis_size("sub") * bases.shape[1]
    )
    identity = jnp.eye(feature_count, dtype=jnp.float32)
    total_gram = lax.psum(local_gram, ("snap", "slab", "sub"))
    r_factor = upper_cholesky(total_gram / cells_total + ridge_value * identity)
    inverse = transposed_solve(r_factor, identity)
    solved = dot_highest(inverse, features)
    whitened = solved.reshape(1, feature_count, layers, columns, -1).astype(jnp.bfloat16)
    return (whitened, r_factor)


def solution(mesh):
    return jax.shard_map(
        local,
        mesh=mesh,
        in_specs=(
            P(("groups", "snap"), None, "slab", "sub", None),
            P(("groups", "snap")),
            P(),
            P(),
            P(),
        ),
        out_specs=(P(("groups", "snap"), None, "slab", "sub", None), P("groups", None)),
        check_vma=False,
    )
```

profile of v0, /device:TPU:0, one launch (start us, length us, event | category | flops | bytes accessed | tf_op | source)
XLA Modules:
  0.0 691.6 jit_solution(17361808163700659640)
XLA Ops:
  7.2 3.0 collective-permute-start.1
  10.3 0.8 bitcast_dynamic-update-slice_fusion.2
  11.1 0.9 slice_bitcast_fusion.7
  12.0 0.9 slice_bitcast_fusion.6
  12.9 0.9 slice_bitcast_fusion.3
  13.9 0.9 slice_bitcast_fusion.2
  15.4 1.3 fusion.15
  16.7 0.8 eq.29
  17.5 0.8 constant_dynamic-update-slice_fusion.1
  18.8 0.7 bitcast_dynamic-update-slice_fusion.1
  20.1 2.1 fusion.8
  22.2 1.0 fusion.6
  23.2 2.1 fusion.17
  25.3 92.5 %all-reduce.2.cloned.1.call-done = f32[192,192]{1,0:T(8,128)} async-done(((f32[192,192]{1,0:T(8,128)}), f32[192,192]{1,0:T(8,128)}) %all-reduce.2.cloned.1.call-update) | async-done | bytes 147472 | tf_op jit(solution)/shard_map/psum | solution.py:109
  117.8 0.9 select_add_fusion
  118.8 288.9 %while.36 = (s32[]{:T(128)}, f32[192,192]{1,0:T(8,128)S(1)}, f32[192,192]{1,0:T(8,128)S(1)}, s32[]{:T(128)}, s32[]{:T(128)}, /*index=5*/s32[]{:T(128)}) while((s32[]{:T(128)}, f32[192,192]{1,0:T(8,128)S(1)}, f32[192,192]{1,0:T(8,128)S(1)}, s32[]{:T(128)}, s32[]{:T(128)}, /*index=5*/s32[]{:T(128)}) %tuple.96), condition=%wide.region_3.4_spmd.clone, body=%wide.region_2.3_spmd.clone.sunk | while | flops 74691 | bytes 302333 | solution.py:49
  407.9 274.4 %while.37 = (s32[]{:T(128)}, f32[192,192]{1,0:T(8,128)S(1)}, f32[192,192]{1,0:T(8,128)S(1)}, f32[192,192]{0,1:T(8,128)S(1)}, s32[]{:T(128)}, /*index=5*/s32[]{:T(128)}, s32[]{:T(128)}) while((s32[]{:T(128)}, f32[192,192]{1,0:T(8,128)S(1)}, f32[192,192]{1,0:T(8,128)S(1)}, f32[192,192]{0,1:T(8,128)S(1)}, s32[]{:T(128)}, ...), condition=%wide.region_5.6_spmd.clone, body=%wide.region_4.5_spmd.clone.sunk | while | flops 443139 | bytes 154493 | solution.py:64
  411.4 0.7 fusion.30
  415.7 0.7 fusion.30
  418.5 0.7 fusion.30
  422.8 0.7 fusion.30
  427.1 0.7 fusion.30
  434.2 0.7 fusion.30
  438.5 0.7 fusion.30
  442.8 0.7 fusion.30
  445.7 0.7 fusion.30
  450.0 0.7 fusion.30
  454.3 0.7 fusion.30
  461.4 0.7 fusion.30
  465.7 0.7 fusion.30
  470.0 0.7 fusion.30
  472.8 0.7 fusion.30
  477.1 0.7 fusion.30
  481.4 0.7 fusion.30
  488.5 0.7 fusion.30
  492.8 0.7 fusion.30
  497.1 0.7 fusion.30
  500.0 0.7 fusion.30
  504.3 0.7 fusion.30
  508.6 0.7 fusion.30
  515.7 0.7 fusion.30
  520.0 0.7 fusion.30
  524.3 0.7 fusion.30
  527.1 0.7 fusion.30
  531.4 0.7 fusion.30
  535.7 0.7 fusion.30
  682.2 1.5 fusion.7
  683.7 1.1 copy.23
  (2112 shorter events, 391.9 us)
Async XLA Ops:
  7.2 12.7 %copy-start = (f32[1,4,2,8,128]{4,3,2,1,0:T(8,128)S(1)}, f32[1,4,2,8,128]{4,3,2,1,0:T(8,128)}, u32[]{:S(2)}) copy-start(f32[1,4,2,8,128]{4,3,2,1,0:T(8,128)} %param.9) | copy-start | bytes 98308
  7.2 110.7 %all-reduce.2.cloned.1.call-start = ((), (), s32[]{:S(2)}) async-start(), calls=%async_computation | async-start | bytes 393216 | tf_op jit(solution)/shard_map/psum | solution.py:109
  7.2 10.2 %collective-permute-start.1 = (f32[1,4,2,8,128]{4,3,2,1,0:T(8,128)}, f32[1,4,2,8,128]{4,3,2,1,0:T(8,128)S(1)}, u32[]{:S(2)}, u32[]{:S(2)}) collective-permute-start(f32[1,4,2,8,128]{4,3,2,1,0:T(8,128)} %param.9), channel_id=1, source_target_pairs={{0,2},{2,0},{1,3},{3,1},{4,6},{6,4},{5,7},{7,5},{8,10},{10,8},{9,1... | collective-permute-start | bytes 98312 | tf_op jit(solution)/shard_map/ppermute | solution.py:15
  10.3 8.0 %collective-permute-start = (f32[1,4,2,8,128]{4,3,2,1,0:T(8,128)}, f32[1,4,2,8,128]{4,3,2,1,0:T(8,128)S(1)}, u32[]{:S(2)}, u32[]{:S(2)}) collective-permute-start(f32[1,4,2,8,128]{4,3,2,1,0:T(8,128)} %param.9), channel_id=1, source_target_pairs={{2,0},{0,2},{3,1},{1,3},{6,4},{4,6},{7,5},{5,7},{10,8},{8,10},{11,... | collective-permute-start | bytes 98312 | tf_op jit(solution)/shard_map/ppermute | solution.py:18
  18.3 1.3 collective-permute-start.2
  18.3 1.3 collective-permute-start.3
  20.1 2.1 copy-start.2
  407.7 276.0 %copy-start.1 = (f32[192,192]{1,0:T(8,128)}, f32[192,192]{1,0:T(8,128)S(1)}, u32[]{:S(2)}) copy-start(f32[192,192]{1,0:T(8,128)S(1)} %get-tuple-element.297) | copy-start | bytes 442372
Sparse Core Ops, SparseCore 0:
  25.4 92.3 all-reduce.1
where the time goes:
time: 696 us; the launch traced here: 692 us
  local copies, waits for them, and re-layouts  254 us (36%)
  loops' own time  151 us (22%)
  matrix products  146 us (21%)
  waiting for transfers between devices  92.6 us (13%)
  other arithmetic  29.2 us (4%)
  between operations  14.9 us (2%)
    dot_general x194, matrix products, dot_highest(): return jnp.dot(left_matrix, right_matrix, precision=lax.Precision.HIGHEST)  144 us
    another operation x1, loops' own time, upper_cholesky(): return lax.fori_loop(0, order, column_step, start)[1]  143 us
    dynamic_slice x192, local copies, waits for them, and re-layouts, row_step(): pivot = lax.dynamic_slice_in_dim(column, step, 1, 0)[0]  114 us
    dynamic_slice x192, local copies, waits for them, and re-layouts, column_step(): pivot = lax.dynamic_slice_in_dim(row_now, step, 1, 0)[0]  113 us
    psum x1, waiting for transfers between devices, local(): total_gram = lax.psum(local_gram, ('snap', 'slab', 'sub'))  92.5 us
    sub x192, other arithmetic, column_step(): work = work - scaled[:, None] * scaled[None, :]  19.5 us
  transfers between devices with their start and end apart: 5, of which 2 were waited for; matrix products, arithmetic and copies ran while one was open for 1% of the time, Pallas kernels for 0%

commit v1 on v0

--- a/solution.py
+++ b/solution.py
@@ -106,7 +106,8 @@
         lax.axis_size("snap") * lax.axis_size("slab") * lax.axis_size("sub") * bases.shape[1]
     )
     identity = jnp.eye(feature_count, dtype=jnp.float32)
-    total_gram = lax.psum(local_gram, ("snap", "slab", "sub"))
+    half = lax.psum(local_gram, ("slab", "sub"))
+    total_gram = lax.psum(half, "snap")
     r_factor = upper_cholesky(total_gram / cells_total + ridge_value * identity)
     inverse = transposed_solve(r_factor, identity)
     solved = dot_highest(inverse, features)

time: 696 us -> 658 us (0.945)
  waiting for transfers between devices: 92.6 us -> 71.2 us
  loops' own time: 151 us -> 135 us
    psum x1 -> x2, waiting for transfers between devices: 92.5 us -> 71.1 us  [the longest x1 37.3 us: local(): total_gram = lax.psum(half, 'snap')]
    another operation x1, loops' own time: 143 us -> 127 us  [upper_cholesky(): return lax.fori_loop(0, order, column_step, start)[1]]
  transfers between devices with their start and end apart: 5 -> 6, of which waited for: 2 -> 3; matrix products, arithmetic and copies ran while one was open for 1% -> 1% of each run, Pallas kernels for 0% -> 0%
where the time goes in v1:
time: 658 us; the launch traced here: 655 us
  local copies, waits for them, and re-layouts  254 us (39%)
  matrix products  146 us (22%)
  loops' own time  135 us (21%)
  waiting for transfers between devices  71.2 us (11%)
  other arithmetic  29.3 us (4%)
  between operations  14.9 us (2%)
    dot_general x194, matrix products, dot_highest(): return jnp.dot(left_matrix, right_matrix, precision=lax.Precision.HIGHEST)  144 us
    another operation x1, loops' own time, upper_cholesky(): return lax.fori_loop(0, order, column_step, start)[1]  127 us
    dynamic_slice x192, local copies, waits for them, and re-layouts, column_step(): pivot = lax.dynamic_slice_in_dim(row_now, step, 1, 0)[0]  114 us
    dynamic_slice x192, local copies, waits for them, and re-layouts, row_step(): pivot = lax.dynamic_slice_in_dim(column, step, 1, 0)[0]  114 us
    psum x1, waiting for transfers between devices, local(): total_gram = lax.psum(half, 'snap')  37.3 us
    psum x1, waiting for transfers between devices, local(): half = lax.psum(local_gram, ('slab', 'sub'))  33.8 us
    sub x192, other arithmetic, column_step(): work = work - scaled[:, None] * scaled[None, :]  19.5 us
  transfers between devices with their start and end apart: 6, of which 3 were waited for; matrix products, arithmetic and copies ran while one was open for 1% of the time, Pallas kernels for 0%

profile of v1, /device:TPU:0, one launch (start us, length us, event | category | flops | bytes accessed | tf_op | source)
XLA Modules:
  0.0 654.6 jit_solution(13722193272102669698)
XLA Ops:
  7.2 3.0 collective-permute-start.1
  10.3 0.8 bitcast_dynamic-update-slice_fusion.2
  11.1 0.9 slice_bitcast_fusion.7
  12.0 0.9 slice_bitcast_fusion.6
  12.9 0.9 slice_bitcast_fusion.3
  13.9 0.9 slice_bitcast_fusion.2
  15.4 1.3 fusion.15
  16.7 0.8 eq.29
  17.5 0.8 constant_dynamic-update-slice_fusion.1
  18.8 0.7 bitcast_dynamic-update-slice_fusion.1
  20.1 2.1 fusion.8
  22.2 1.1 fusion.6
  23.3 2.1 fusion.17
  25.5 33.8 %all-reduce.3.cloned.1.call-done = f32[192,192]{1,0:T(8,128)} async-done(((f32[192,192]{1,0:T(8,128)}), f32[192,192]{1,0:T(8,128)}) %all-reduce.3.cloned.1.call-update) | async-done | bytes 147472 | tf_op jit(solution)/shard_map/psum | solution.py:109
  59.3 37.3 %all-reduce.5.cloned.1.call-done = f32[192,192]{1,0:T(8,128)} async-done(((f32[192,192]{1,0:T(8,128)}), f32[192,192]{1,0:T(8,128)}) %all-reduce.5.cloned.1.call-update) | async-done | bytes 147472 | tf_op jit(solution)/shard_map/psum | solution.py:110
  96.6 0.9 select_add_fusion
  97.6 273.1 %while.36 = (s32[]{:T(128)}, f32[192,192]{1,0:T(8,128)S(1)}, f32[192,192]{1,0:T(8,128)S(1)}, s32[]{:T(128)}, s32[]{:T(128)}, /*index=5*/s32[]{:T(128)}) while((s32[]{:T(128)}, f32[192,192]{1,0:T(8,128)S(1)}, f32[192,192]{1,0:T(8,128)S(1)}, s32[]{:T(128)}, s32[]{:T(128)}, /*index=5*/s32[]{:T(128)}) %tuple.96), condition=%wide.region_4.5_spmd.clone, body=%wide.region_3.4_spmd.clone.sunk | while | flops 74691 | bytes 302333 | solution.py:49
  370.9 274.4 %while.37 = (s32[]{:T(128)}, f32[192,192]{1,0:T(8,128)S(1)}, f32[192,192]{1,0:T(8,128)S(1)}, f32[192,192]{0,1:T(8,128)S(1)}, s32[]{:T(128)}, /*index=5*/s32[]{:T(128)}, s32[]{:T(128)}) while((s32[]{:T(128)}, f32[192,192]{1,0:T(8,128)S(1)}, f32[192,192]{1,0:T(8,128)S(1)}, f32[192,192]{0,1:T(8,128)S(1)}, s32[]{:T(128)}, ...), condition=%wide.region_6.7_spmd.clone, body=%wide.region_5.6_spmd.clone.sunk | while | flops 443139 | bytes 154493 | solution.py:64
  371.5 0.7 fusion.30
  375.8 0.7 fusion.30
  380.1 0.7 fusion.30
  383.0 0.7 fusion.30
  387.2 0.7 fusion.30
  391.5 0.7 fusion.30
  398.7 0.7 fusion.30
  403.0 0.7 fusion.30
  407.3 0.7 fusion.30
  410.1 0.7 fusion.30
  414.4 0.7 fusion.30
  418.7 0.7 fusion.30
  425.8 0.7 fusion.30
  430.1 0.7 fusion.30
  434.4 0.7 fusion.30
  437.3 0.7 fusion.30
  441.5 0.7 fusion.30
  445.8 0.7 fusion.30
  453.0 0.7 fusion.30
  457.3 0.7 fusion.30
  461.6 0.7 fusion.30
  464.4 0.7 fusion.30
  468.7 0.7 fusion.30
  473.0 0.7 fusion.30
  480.1 0.7 fusion.30
  484.4 0.7 fusion.30
  488.7 0.7 fusion.30
  491.6 0.7 fusion.30
  645.3 1.5 fusion.7
  646.7 1.1 copy.23
  (2115 shorter events, 393.2 us)
Async XLA Ops:
  7.2 12.7 %copy-start = (f32[1,4,2,8,128]{4,3,2,1,0:T(8,128)S(1)}, f32[1,4,2,8,128]{4,3,2,1,0:T(8,128)}, u32[]{:S(2)}) copy-start(f32[1,4,2,8,128]{4,3,2,1,0:T(8,128)} %param.9) | copy-start | bytes 98308
  7.2 52.1 %all-reduce.3.cloned.1.call-start = ((), (), s32[]{:S(2)}) async-start(), calls=%async_computation | async-start | bytes 393216 | tf_op jit(solution)/shard_map/psum | solution.py:109
  7.2 10.2 %collective-permute-start.1 = (f32[1,4,2,8,128]{4,3,2,1,0:T(8,128)}, f32[1,4,2,8,128]{4,3,2,1,0:T(8,128)S(1)}, u32[]{:S(2)}, u32[]{:S(2)}) collective-permute-start(f32[1,4,2,8,128]{4,3,2,1,0:T(8,128)} %param.9), channel_id=1, source_target_pairs={{0,2},{2,0},{1,3},{3,1},{4,6},{6,4},{5,7},{7,5},{8,10},{10,8},{9,1... | collective-permute-start | bytes 98312 | tf_op jit(solution)/shard_map/ppermute | solution.py:15
  10.3 8.0 %collective-permute-start = (f32[1,4,2,8,128]{4,3,2,1,0:T(8,128)}, f32[1,4,2,8,128]{4,3,2,1,0:T(8,128)S(1)}, u32[]{:S(2)}, u32[]{:S(2)}) collective-permute-start(f32[1,4,2,8,128]{4,3,2,1,0:T(8,128)} %param.9), channel_id=1, source_target_pairs={{2,0},{0,2},{3,1},{1,3},{6,4},{4,6},{7,5},{5,7},{10,8},{8,10},{11,... | collective-permute-start | bytes 98312 | tf_op jit(solution)/shard_map/ppermute | solution.py:18
  18.3 1.3 collective-permute-start.2
  18.3 1.3 collective-permute-start.3
  20.1 2.1 copy-start.2
  25.4 71.2 %all-reduce.5.cloned.1.call-start = ((), (), s32[]{:S(2)}) async-start(), calls=%async_computation.1 | async-start | bytes 393216 | tf_op jit(solution)/shard_map/psum | solution.py:110
  370.7 276.0 %copy-start.1 = (f32[192,192]{1,0:T(8,128)}, f32[192,192]{1,0:T(8,128)S(1)}, u32[]{:S(2)}) copy-start(f32[192,192]{1,0:T(8,128)S(1)} %get-tuple-element.297) | copy-start | bytes 442372
Sparse Core Ops, SparseCore 0:
  25.5 33.6 all-reduce.2
  61.6 34.9 all-reduce.4

commit v2 on v0

--- a/solution.py
+++ b/solution.py
@@ -106,7 +106,8 @@
         lax.axis_size("snap") * lax.axis_size("slab") * lax.axis_size("sub") * bases.shape[1]
     )
     identity = jnp.eye(feature_count, dtype=jnp.float32)
-    total_gram = lax.psum(local_gram, ("snap", "slab", "sub"))
+    blocks = lax.all_gather(local_gram, ("snap", "slab", "sub"), axis=0, tiled=False)
+    total_gram = blocks.sum(axis=0)
     r_factor = upper_cholesky(total_gram / cells_total + ridge_value * identity)
     inverse = transposed_solve(r_factor, identity)
     solved = dot_highest(inverse, features)

time: 696 us -> 652 us (0.937)
  waiting for transfers between devices: 92.6 us -> 47.4 us
    psum x1 -> x0, waiting for transfers between devices: 92.5 us -> none  [local(): total_gram = lax.psum(local_gram, ('snap', 'slab', 'sub'))]
    all_gather x0 -> x1, waiting for transfers between devices: none -> 47.3 us  [local(): lax.all_gather(local_gram, ('snap', 'slab', 'sub'), axis=0, tiled=False)]
where the time goes in v2:
time: 652 us; the launch traced here: 648 us
  local copies, waits for them, and re-layouts  254 us (39%)
  loops' own time  151 us (23%)
  matrix products  146 us (22%)
  waiting for transfers between devices  47.4 us (7%)
  other arithmetic  30.5 us (5%)
  between operations  14.9 us (2%)
    dot_general x194, matrix products, dot_highest(): return jnp.dot(left_matrix, right_matrix, precision=lax.Precision.HIGHEST)  144 us
    another operation x1, loops' own time, upper_cholesky(): return lax.fori_loop(0, order, column_step, start)[1]  143 us
    dynamic_slice x192, local copies, waits for them, and re-layouts, row_step(): pivot = lax.dynamic_slice_in_dim(column, step, 1, 0)[0]  114 us
    dynamic_slice x192, local copies, waits for them, and re-layouts, column_step(): pivot = lax.dynamic_slice_in_dim(row_now, step, 1, 0)[0]  113 us
    all_gather x1, waiting for transfers between devices, local(): lax.all_gather(local_gram, ('snap', 'slab', 'sub'), axis=0, tiled=False)  47.3 us
    sub x192, other arithmetic, column_step(): work = work - scaled[:, None] * scaled[None, :]  19.5 us
  transfers between devices with their start and end apart: 5, of which 2 were waited for; matrix products, arithmetic and copies ran while one was open for 1% of the time, Pallas kernels for 0%

profile of v2, /device:TPU:0, one launch (start us, length us, event | category | flops | bytes accessed | tf_op | source)
XLA Modules:
  0.0 647.7 jit_solution(13571493129565778613)
XLA Ops:
  7.2 3.0 collective-permute-start.1
  10.3 0.8 bitcast_dynamic-update-slice_fusion.2
  11.1 0.9 slice_bitcast_fusion.7
  12.0 0.9 slice_bitcast_fusion.6
  12.9 0.9 slice_bitcast_fusion.3
  13.9 0.9 slice_bitcast_fusion.2
  15.4 1.3 fusion.15
  16.7 0.8 eq.29
  17.5 0.8 constant_dynamic-update-slice_fusion.1
  18.8 0.7 bitcast_dynamic-update-slice_fusion.1
  20.1 2.1 fusion.8
  22.2 1.1 fusion.6
  23.3 2.1 fusion.17
  25.4 47.3 %all-gather.3.cloned.1.call-done = f32[3072,192]{1,0:T(8,128)} async-done(((f32[192,192]{1,0:T(8,128)}), f32[3072,192]{1,0:T(8,128)}) %all-gather.3.cloned.1.call-update) | async-done | bytes 2359312 | tf_op jit(solution)/shard_map/all_gather | solution.py:109
  72.7 2.1 reduce_sum.19
  74.9 288.9 %while.36 = (s32[]{:T(128)}, f32[192,192]{1,0:T(8,128)S(1)}, f32[192,192]{1,0:T(8,128)S(1)}, s32[]{:T(128)}, s32[]{:T(128)}, /*index=5*/s32[]{:T(128)}) while((s32[]{:T(128)}, f32[192,192]{1,0:T(8,128)S(1)}, f32[192,192]{1,0:T(8,128)S(1)}, s32[]{:T(128)}, s32[]{:T(128)}, /*index=5*/s32[]{:T(128)}) %tuple.96), condition=%wide.region_3.4_spmd.clone, body=%wide.region_2.3_spmd.clone.sunk | while | flops 74691 | bytes 302333 | solution.py:49
  364.0 274.4 %while.37 = (s32[]{:T(128)}, f32[192,192]{1,0:T(8,128)S(1)}, f32[192,192]{1,0:T(8,128)S(1)}, f32[192,192]{0,1:T(8,128)S(1)}, s32[]{:T(128)}, /*index=5*/s32[]{:T(128)}, s32[]{:T(128)}) while((s32[]{:T(128)}, f32[192,192]{1,0:T(8,128)S(1)}, f32[192,192]{1,0:T(8,128)S(1)}, f32[192,192]{0,1:T(8,128)S(1)}, s32[]{:T(128)}, ...), condition=%wide.region_5.6_spmd.clone, body=%wide.region_4.5_spmd.clone.sunk | while | flops 443139 | bytes 154493 | solution.py:64
  366.0 0.7 fusion.30
  368.9 0.7 fusion.30
  373.2 0.7 fusion.30
  377.5 0.7 fusion.30
  384.6 0.7 fusion.30
  388.9 0.7 fusion.30
  393.2 0.7 fusion.30
  396.0 0.7 fusion.30
  400.3 0.7 fusion.30
  404.6 0.7 fusion.30
  411.8 0.7 fusion.30
  416.1 0.7 fusion.30
  420.3 0.7 fusion.30
  423.2 0.7 fusion.30
  427.5 0.7 fusion.30
  431.8 0.7 fusion.30
  438.9 0.7 fusion.30
  443.2 0.7 fusion.30
  447.5 0.7 fusion.30
  450.3 0.7 fusion.30
  454.6 0.7 fusion.30
  458.9 0.7 fusion.30
  466.1 0.7 fusion.30
  470.4 0.7 fusion.30
  474.6 0.7 fusion.30
  477.5 0.7 fusion.30
  481.8 0.7 fusion.30
  486.1 0.7 fusion.30
  493.2 0.7 fusion.30
  638.3 1.5 fusion.7
  639.8 1.1 copy.23
  (2113 shorter events, 392.0 us)
Async XLA Ops:
  7.2 12.7 %copy-start = (f32[1,4,2,8,128]{4,3,2,1,0:T(8,128)S(1)}, f32[1,4,2,8,128]{4,3,2,1,0:T(8,128)}, u32[]{:S(2)}) copy-start(f32[1,4,2,8,128]{4,3,2,1,0:T(8,128)} %param.9) | copy-start | bytes 98308
  7.2 65.5 %all-gather.3.cloned.1.call-start = ((), (), s32[]{:S(2)}) async-start(), calls=%async_computation | async-start | bytes 3342336 | tf_op jit(solution)/shard_map/all_gather | solution.py:109
  7.2 10.2 %collective-permute-start.1 = (f32[1,4,2,8,128]{4,3,2,1,0:T(8,128)}, f32[1,4,2,8,128]{4,3,2,1,0:T(8,128)S(1)}, u32[]{:S(2)}, u32[]{:S(2)}) collective-permute-start(f32[1,4,2,8,128]{4,3,2,1,0:T(8,128)} %param.9), channel_id=1, source_target_pairs={{0,2},{2,0},{1,3},{3,1},{4,6},{6,4},{5,7},{7,5},{8,10},{10,8},{9,1... | collective-permute-start | bytes 98312 | tf_op jit(solution)/shard_map/ppermute | solution.py:15
  10.3 8.0 %collective-permute-start = (f32[1,4,2,8,128]{4,3,2,1,0:T(8,128)}, f32[1,4,2,8,128]{4,3,2,1,0:T(8,128)S(1)}, u32[]{:S(2)}, u32[]{:S(2)}) collective-permute-start(f32[1,4,2,8,128]{4,3,2,1,0:T(8,128)} %param.9), channel_id=1, source_target_pairs={{2,0},{0,2},{3,1},{1,3},{6,4},{4,6},{7,5},{5,7},{10,8},{8,10},{11,... | collective-permute-start | bytes 98312 | tf_op jit(solution)/shard_map/ppermute | solution.py:18
  18.3 1.3 collective-permute-start.2
  18.3 1.3 collective-permute-start.3
  20.1 2.1 copy-start.2
  363.8 276.0 %copy-start.1 = (f32[192,192]{1,0:T(8,128)}, f32[192,192]{1,0:T(8,128)S(1)}, u32[]{:S(2)}) copy-start(f32[192,192]{1,0:T(8,128)S(1)} %get-tuple-element.297) | copy-start | bytes 442372
Sparse Core Ops, SparseCore 0:
  25.5 47.1 all-gather.2
